TPU v7x, 32 devices: a whole 2x2x4 slice. The times are simulated.
32 devices in a mesh: space: 16 (over z, y, x), tm: 2 (over core).
Axes of the slice: x: 2, y: 2, z: 4, core: 2. Of those that a mesh axis runs over, the one named last changes fastest.
Arguments:
- snapshots: bfloat16 [131072, 128], P('space', 'tm'), may hold values from -6 to 6
- basis: bfloat16 [131072, 192], P('space'), may hold values from -0.015625 to 0.015625
- tile_slots: int32 [704], P(('space', 'tm')), may hold values from 0 to 703, each once
Outputs:
- gram_tiles: float32 [704, 512, 512], P(('space', 'tm'))
Inputs may be any that keep to these rules, and one draw needn't show every extreme that they name: `tile_slots`: every tile number below 703 stands in exactly one slot; the other values mark empty slots.
All inputs are finite; a program needn't handle non-finite values.
Results may differ from a plain program's by a relative error of at most 0.0039.
Values sent between devices are 32-bit elements; how exact they have to be, the bound alone decides.
A program may use at most 128 MiB of HBM per device.

v0:
```python
import jax
import jax.numpy as jnp
import numpy as np
from jax import lax
from jax.sharding import PartitionSpec as P

R = 192
BLK = 512
NB = 37
NTILE = 703


def pair_tables():
    first = []
    second = []
    for k in range(R):
        first.append(k)
        second.append(R)
    for i in range(R):
        for j in range(i, R):
            first.append(i)
            second.append(j)
    while len(first) < NB * BLK:
        first.append(R + 1)
        second.append(R + 1)
    return (
        np.array(first, dtype=np.int32).reshape(NB, BLK),
        np.array(second, dtype=np.int32).reshape(NB, BLK),
    )


def tile_tables():
    rows_list = []
    cols_list = []
    for a in range(NB):
        for b in range(a + 1):
            rows_list.append(a)
            cols_list.append(b)
    return (np.array(rows_list, dtype=np.int32), np.array(cols_list, dtype=np.int32))


def body(snapshots, basis, tile_slots):
    partial_value = jnp.dot(basis.T, snapshots, preferred_element_type=jnp.float32)
    coeffs = lax.psum(partial_value, "space")
    total_steps = snapshots.shape[1] * lax.axis_size("tm")
    tile_row, tile_col = tile_tables()
    valid = tile_slots < NTILE
    index = jnp.minimum(tile_slots, NTILE - 1)
    onehot = (index[:, None] == jnp.arange(NTILE, dtype=jnp.int32)[None, :]).astype(jnp.int32)
    block_a = jnp.sum(onehot * jnp.asarray(tile_row)[None, :], axis=1)
    block_b = jnp.sum(onehot * jnp.asarray(tile_col)[None, :], axis=1)
    first, second = pair_tables()
    first = jnp.asarray(first)
    second = jnp.asarray(second)
    left_one = jnp.take(first, block_a, axis=0)
    left_two = jnp.take(second, block_a, axis=0)
    right_one = jnp.take(first, block_b, axis=0)
    right_two = jnp.take(second, block_b, axis=0)
    piece = lax.all_gather(coeffs, "tm", axis=1, tiled=True)
    width = piece.shape[1]
    extended = jnp.concatenate(
        [piece, jnp.ones((1, width), jnp.float32), jnp.zeros((1, width), jnp.float32)], axis=0
    )
    left_feat = (
        jnp.take(extended, left_one, axis=0) * jnp.take(extended, left_two, axis=0)
    ).astype(jnp.bfloat16)
    right_feat = (
        jnp.take(extended, right_one, axis=0) * jnp.take(extended, right_two, axis=0)
    ).astype(jnp.bfloat16)
    summed = jnp.einsum("sic,sjc->sij", left_feat, right_feat, preferred_element_type=jnp.float32)
    scale = valid.astype(jnp.float32) / total_steps
    return summed * scale[:, None, None]


def solution(mesh):
    in_specs = (P("space", "tm"), P("space", None), P(("space", "tm")))
    out_specs = P(("space", "tm"), None, None)
    return jax.shard_map(body, mesh=mesh, in_specs=in_specs, out_specs=out_specs, check_vma=False)
```

profile of v0, /device:TPU:0, one launch (start us, length us, event | category | flops | bytes accessed | tf_op | source)
XLA Modules:
  0.0 267.1 jit_solution(8727437364808275942)
XLA Ops:
  0.0 0.0 copy-start
  0.0 0.8 compare_select_fusion.6
  0.8 0.8 broadcast_minimum_fusion
  1.6 0.9 select_reduce_fusion
  2.5 0.7 pad.1.clone
  3.2 0.7 pad.2.clone
  3.9 1.5 gather_fusion.2
  5.4 1.5 gather_fusion
  6.9 0.1 compare_and_fusion.3
  7.1 1.5 gather_fusion.6
  8.6 1.5 gather_fusion.4
  10.1 0.7 compare_and_fusion.1
  10.8 0.6 broadcast_clamp_fusion
  11.4 0.0 copy-done
  11.4 2.3 fusion.10
  13.8 78.6 %psum.7 = f32[192,64]{0,1:T(8,128)S(1)} all-reduce(f32[192,64]{0,1:T(8,128)S(1)} %fusion.10), channel_id=1, replica_groups=mesh['space'=16,'tm'=2] {'space'}, use_global_device_ids=true, to_apply=%region_0.0 | all-reduce | flops 12288 | bytes 98304 | tf_op jit(solution)/shard_map/psum | solution.py:44
  92.4 1.9 all_gather.3
  94.3 0.7 maximum_maximum_fusion
  95.0 0.1 copy.12
  95.1 41.4 %gather_fusion.7 = f32[11264,128]{1,0:T(8,128)} fusion(f32[194,128]{1,0:T(8,128)S(1)} %copy.12, s32[11264]{0:T(1024)} %broadcast_clamp_fusion), kind=kCustom, calls=%fused_computation.7.clone | custom fusion | bytes 11579392 | tf_op jit(solution)/shard_map/jit(_take)/gather | solution.py:68
  136.5 37.7 %gather_fusion.5 = f32[11264,128]{1,0:T(8,128)} fusion(f32[194,128]{1,0:T(8,128)S(1)} %copy.12, s32[11264]{0:T(1024)S(1)} %broadcast_clamp_fusion.1), kind=kCustom, calls=%fused_computation.6.clone | custom fusion | bytes 11579392 | tf_op jit(solution)/shard_map/jit(_take)/gather | solution.py:68
  174.3 37.8 %gather_fusion.3 = f32[11264,128]{1,0:T(8,128)} fusion(f32[194,128]{1,0:T(8,128)S(1)} %copy.12, s32[11264]{0:T(1024)S(1)} %broadcast_clamp_fusion.2), kind=kCustom, calls=%fused_computation.5.clone | custom fusion | bytes 11579392 | tf_op jit(solution)/shard_map/jit(_take)/gather | solution.py:65
  212.0 0.0 copy-start.1
  212.0 37.8 %gather_fusion.1 = f32[11264,128]{1,0:T(8,128)} fusion(f32[194,128]{1,0:T(8,128)S(1)} %copy.12, s32[11264]{0:T(1024)S(1)} %broadcast_clamp_fusion.3), kind=kCustom, calls=%fused_computation.1.clone | custom fusion | bytes 11579392 | tf_op jit(solution)/shard_map/jit(_take)/gather | solution.py:65
  249.8 0.0 copy-done.1
  249.8 17.2 %broadcast_multiply_fusion = f32[22,512,512]{2,1,0:T(8,128)} fusion(f32[22]{0:T(128)S(1)} %compare_select_fusion.6, f32[22,512,128]{2,1,0:T(8,128)} %bitcast.10, f32[22,512,128]{2,1,0:T(8,128)} %bitcast.11, f32[22,512,128]{2,1,0:T(8,128)} %bitcast.8, f32[22,512,128]{2,1,0:T(8,128)} %bitcast.9, pred[22,512]{1,0:T(8,128)(4,1)S(1)} %copy-done.1, ...), kind=kOutput, calls=%fused_computation.8 | convolution fusion | flops 1493696512 | bytes 46182488 | tf_op jit(solution)/shard_map/sic,sjc->sij/dot_general | solution.py:70
  (11 shorter events, 0.1 us)
Async XLA Ops:
  0.0 11.4 %copy-start = (bf16[8192,192]{0,1:T(8,128)(2,1)S(1)}, bf16[8192,192]{0,1:T(8,128)(2,1)}, u32[]{:S(2)}) copy-start(bf16[8192,192]{0,1:T(8,128)(2,1)} %param.12) | copy-start | bytes 9437188
  212.0 37.8 %copy-start.1 = (pred[22,512]{1,0:T(8,128)(4,1)S(1)}, pred[22,512]{1,0:T(8,128)(4,1)}, u32[]{:S(2)}) copy-start(pred[22,512]{1,0:T(8,128)(4,1)} %get-tuple-element.17) | copy-start | bytes 33796
where the time goes:
time: 268 us; the launch traced here: 267 us
  local copies, waits for them, and re-layouts  162 us (60%)
  blocking collectives  80.5 us (30%)
  matrix products  19.6 us (7%)
  other arithmetic  4.7 us (2%)
    psum x1, blocking collectives, body(): coeffs = lax.psum(partial_value, 'space')  78.6 us
    gather x1, local copies, waits for them, and re-layouts, body(): jnp.take(extended, right_two, axis=0)  41.4 us
    gather x1, local copies, waits for them, and re-layouts, body(): jnp.take(extended, left_one, axis=0) * jnp.take(extended, left_two, axis=0)  37.8 us
    gather x1, local copies, waits for them, and re-layouts, body(): jnp.take(extended, left_two, axis=0)  37.8 us
    gather x1, local copies, waits for them, and re-layouts, body(): jnp.take(extended, right_one, axis=0)  37.7 us
    dot_general x1, matrix products, body(): jnp.einsum('sic,sjc->sij', left_feat, right_feat, preferred_element_type=...  17.2 us

commit v1 on v0

v1 whole, which is shorter than its diff:
```python
import functools

import jax
import jax.numpy as jnp
from jax import lax
from jax.experimental import pallas as pl
from jax.experimental.pallas import tpu as pltpu
from jax.sharding import PartitionSpec as P

R = 192
BLK = 512
NB = 37
NTILE = NB * (NB + 1) // 2
HALF = R // 2
LANES = 128
MESH = pl.DeviceIdType.MESH

NT_DIMS = (((1,), (1,)), ((), ()))


def segment_starts():
    starts, at = [], R
    for i in range(R):
        starts.append(at)
        at += R - i
    return starts, at


def coeff_kernel(
    n, tm, chunks, basis_ref, snap_ref, out_ref,
    bas, snp, whole, part, recv, gath, flat,
    bas_sem, snp_sem, send1, recv1, send2, recv2,
):
    total = n * tm
    s = lax.axis_index("space")
    t = lax.axis_index("tm")
    me = s * tm + t
    width = snap_ref.shape[0]
    depth = basis_ref.shape[1] // chunks
    rows = HALF // n

    loads = []
    for k in range(chunks):
        at = pl.ds(k * depth, depth)
        one = pltpu.make_async_copy(basis_ref.at[:, at], bas.at[k], bas_sem.at[k])
        two = pltpu.make_async_copy(snap_ref.at[:, at], snp.at[k], snp_sem.at[k])
        one.start()
        two.start()
        loads.append((one, two))

    barrier = pltpu.get_barrier_semaphore()

    def greet(d, carry):
        peer = lax.rem(me + d, total)
        pl.semaphore_signal(
            barrier, inc=1,
            device_id={"space": lax.div(peer, tm), "tm": lax.rem(peer, tm)},
            device_id_type=MESH,
        )
        return carry

    lax.fori_loop(1, total, greet, 0)

    acc = jnp.zeros((R, width), jnp.float32)
    for k in range(chunks):
        loads[k][0].wait()
        loads[k][1].wait()
        acc = acc + lax.dot_general(
            bas[k], snp[k], NT_DIMS, preferred_element_type=jnp.float32
        )
    whole[...] = jnp.concatenate([acc[:HALF], acc[HALF:]], axis=1)
    for q in range(n):
        part[q] = whole[q * rows:(q + 1) * rows, :]

    pl.semaphore_wait(barrier, total - 1)

    def scatter(d):
        dst = lax.rem(s + d, n)
        return pltpu.make_async_remote_copy(
            src_ref=part.at[dst], dst_ref=recv.at[d],
            send_sem=send1.at[d], recv_sem=recv1.at[d],
            device_id={"space": dst, "tm": t}, device_id_type=MESH,
        )

    def start_scatter(d, carry):
        scatter(d).start()
        return carry

    lax.fori_loop(1, n, start_scatter, 0)

    def add(d, value):
        scatter(d).wait_recv()
        return value + recv[d]

    gath[t, s] = lax.fori_loop(1, n, add, part[s])

    def gather(d):
        peer = lax.rem(me + d, total)
        return pltpu.make_async_remote_copy(
            src_ref=gath.at[t, s], dst_ref=gath.at[t, s],
            send_sem=send2.at[d], recv_sem=recv2.at[d],
            device_id={"space": lax.div(peer, tm), "tm": lax.rem(peer, tm)},
            device_id_type=MESH,
        )

    def start_gather(d, carry):
        gather(d).start()
        return carry

    lax.fori_loop(1, total, start_gather, 0)

    def end_scatter(d, carry):
        scatter(d).wait_send()
        return carry

    lax.fori_loop(1, n, end_scatter, 0)

    def end_gather(d, carry):
        gather(d).wait_recv()
        return carry

    lax.fori_loop(1, total, end_gather, 0)

    for u in range(tm):
        for q in range(n):
            flat[u, q * rows:(q + 1) * rows, :] = gath[u, q]
    per = LANES // width
    for v in range(tm // per):
        blocks = [flat[v * per + u] for u in range(per)]
        for h in range(2):
            out_ref[v, h * HALF:(h + 1) * HALF, :] = jnp.concatenate(
                [b[:, h * width:(h + 1) * width] for b in blocks], axis=1
            )

    def end_send(d, carry):
        gather(d).wait_send()
        return carry

    lax.fori_loop(1, total, end_send, 0)


def coefficients(n, tm, basis_t, snap_t):
    width, cells = snap_t.shape
    chunks = 4
    depth = cells // chunks
    total = n * tm
    rows = HALF // n
    blocks = tm * width // LANES
    return pl.pallas_call(
        functools.partial(coeff_kernel, n, tm, chunks),
        out_shape=jax.ShapeDtypeStruct((blocks, R, LANES), jnp.float32),
        in_specs=[pl.BlockSpec(memory_space=pl.ANY)] * 2,
        out_specs=pl.BlockSpec(memory_space=pltpu.VMEM),
        scratch_shapes=[
            pltpu.VMEM((chunks, R, depth), jnp.bfloat16),
            pltpu.VMEM((chunks, width, depth), jnp.bfloat16),
            pltpu.VMEM((HALF, LANES), jnp.float32),
            pltpu.VMEM((n, rows, LANES), jnp.float32),
            pltpu.VMEM((n, rows, LANES), jnp.float32),
            pltpu.VMEM((tm, n, rows, LANES), jnp.float32),
            pltpu.VMEM((tm, HALF, LANES), jnp.float32),
            pltpu.SemaphoreType.DMA((chunks,)),
            pltpu.SemaphoreType.DMA((chunks,)),
            pltpu.SemaphoreType.DMA((n,)),
            pltpu.SemaphoreType.DMA((n,)),
            pltpu.SemaphoreType.DMA((total,)),
            pltpu.SemaphoreType.DMA((total,)),
        ],
        compiler_params=pltpu.CompilerParams(collective_id=0, has_side_effects=True),
        name="coeffs",
    )(basis_t, snap_t)


def tile_kernel(slots_ref, coeff_ref, out_ref, wide, feats, tiles, sems):
    blocks = coeff_ref.shape[0]
    slots = out_ref.shape[0]
    steps = blocks * LANES
    starts, end = segment_starts()

    for v in range(blocks):
        wide[v, :R, :] = coeff_ref[v]
        wide[v, R:, :] = jnp.zeros((8, LANES), jnp.float32)
        feats[v, end:, :] = jnp.zeros((feats.shape[1] - end, LANES), jnp.float32)

    @pl.loop(0, blocks)
    def _(v):
        feats[v, :R, :] = wide[v, :R, :]
        for i in range(R):
            size = R - i
            feats[v, starts[i]:starts[i] + size, :] = (
                wide[v, i:i + size, :] * wide[v, i:i + 1, :]
            )

    def copy(k):
        return pltpu.make_async_copy(tiles.at[k], out_ref.at[k], sems.at[k])

    @pl.loop(0, slots)
    def _(k):
        slot = slots_ref[k]
        index = jnp.minimum(slot, NTILE - 1)
        a = jnp.int32(0)
        for m in range(1, NB):
            a = a + (index >= m * (m + 1) // 2).astype(jnp.int32)
        b = index - lax.div(a * (a + 1), 2)
        scale = jnp.where(slot < NTILE, jnp.float32(1.0 / steps), jnp.float32(0.0))
        left_at = pl.ds(pl.multiple_of(a * BLK, BLK), BLK)
        right_at = pl.ds(pl.multiple_of(b * BLK, BLK), BLK)
        out = None
        for v in range(blocks):
            left = feats[v, left_at, :].astype(jnp.bfloat16)
            right = feats[v, right_at, :].astype(jnp.bfloat16)
            one = lax.dot_general(left, right, NT_DIMS, preferred_element_type=jnp.float32)
            out = one if out is None else out + one
        tiles[k] = out * scale
        copy(k).start()

    @pl.loop(0, slots)
    def _(k):
        copy(k).wait()


def gram(tile_slots, coeffs):
    slots = tile_slots.shape[0]
    blocks = coeffs.shape[0]
    return pl.pallas_call(
        tile_kernel,
        out_shape=jax.ShapeDtypeStruct((slots, BLK, BLK), jnp.float32),
        in_specs=[
            pl.BlockSpec(memory_space=pltpu.SMEM),
            pl.BlockSpec(memory_space=pltpu.VMEM),
        ],
        out_specs=pl.BlockSpec(memory_space=pl.ANY),
        scratch_shapes=[
            pltpu.VMEM((blocks, R + 8, LANES), jnp.float32),
            pltpu.VMEM((blocks, NB * BLK, LANES), jnp.float32),
            pltpu.VMEM((slots, BLK, BLK), jnp.float32),
            pltpu.SemaphoreType.DMA((slots,)),
        ],
        compiler_params=pltpu.CompilerParams(vmem_limit_bytes=56 << 20),
        name="tiles",
    )(tile_slots, coeffs)


def body(n, tm, snapshots, basis, tile_slots):
    coeffs = coefficients(n, tm, basis.T, snapshots.T)
    return gram(tile_slots, coeffs)


def solution(mesh):
    n, tm = mesh.shape["space"], mesh.shape["tm"]
    in_specs = (P("space", "tm"), P("space", None), P(("space", "tm")))
    out_specs = P(("space", "tm"), None, None)
    return jax.shard_map(
        functools.partial(body, n, tm), mesh=mesh,
        in_specs=in_specs, out_specs=out_specs, check_vma=False,
    )
```

time: 268 us -> 28.5 us (0.11)
  local copies, waits for them, and re-layouts: 162 us -> 0 us
  blocking collectives: 80.5 us -> 0 us
  Pallas kernels: 0 us -> 28.3 us
  matrix products: 19.6 us -> 0 us
  other arithmetic: 4.7 us -> 0 us
    gather x8 -> x0, local copies, waits for them, and re-layouts: 161 us -> none  [the longest x1 41.4 us: body(): jnp.take(extended, right_two, axis=0)]
    psum x1 -> x0, blocking collectives: 78.6 us -> none  [body(): coeffs = lax.psum(partial_value, 'space')]
    pallas_call x0 -> x2, Pallas kernels: none -> 28.3 us  [the longest x1 18.1 us: coefficients(): pl.pallas_call(functools.partial(coeff_kernel, n, tm, chunks), out_shape=...]
    dot_general x2 -> x0, matrix products: 19.6 us -> none  [the longest x1 17.2 us: body(): jnp.einsum('sic,sjc->sij', left_feat, right_feat, preferred_element_type=...]
where the time goes in v1:
time: 28.5 us; the launch traced here: 28.3 us
  Pallas kernels  28.3 us (99%)
    pallas_call x1, Pallas kernels, coefficients(): pl.pallas_call(functools.partial(coeff_kernel, n, tm, chunks), out_shape=...  18.1 us
    pallas_call x1, Pallas kernels, gram(): pl.pallas_call(tile_kernel, out_shape=jax.ShapeDtypeStruct((slots, BLK, B...  10.2 us

profile of v1, /device:TPU:0, one launch (start us, length us, event | category | flops | bytes accessed | tf_op | source)
XLA Modules:
  0.0 28.3 jit_solution(14856670642257588170)
XLA Ops:
  0.0 18.1 %coeffs.1.coeff_ref = f32[1,192,128]{2,1,0:T(8,128)} custom-call(bf16[192,8192]{1,0:T(8,128)(2,1)} %bitcast.2, bf16[64,8192]{1,0:T(8,128)(2,1)} %bitcast.3), custom_call_target="tpu_custom_call" | custom-call | tf_op jit(solution)/shard_map/coeffs/pallas_call | solution.py:149
  18.1 10.2 %tiles.1 = f32[22,512,512]{2,1,0:T(8,128)} custom-call(s32[22]{0:T(128)} %slots_ref.1, f32[1,192,128]{2,1,0:T(8,128)} %coeffs.1.coeff_ref), custom_call_target="tpu_custom_call" | custom-call | tf_op jit(solution)/shard_map/tiles/pallas_call | solution.py:225

commit v2 on v1

--- a/solution.py
+++ b/solution.py
@@ -141,14 +141,14 @@
 
 def coefficients(n, tm, basis_t, snap_t):
     width, cells = snap_t.shape
-    chunks = 4
+    chunks = 2
     depth = cells // chunks
     total = n * tm
     rows = HALF // n
     blocks = tm * width // LANES
     return pl.pallas_call(
         functools.partial(coeff_kernel, n, tm, chunks),
-        out_shape=jax.ShapeDtypeStruct((blocks, R, LANES), jnp.float32),
+        out_shape=pltpu.VMEM((blocks, R, LANES), jnp.float32),
         in_specs=[pl.BlockSpec(memory_space=pl.ANY)] * 2,
         out_specs=pl.BlockSpec(memory_space=pltpu.VMEM),
         scratch_shapes=[
@@ -194,7 +194,7 @@
     def copy(k):
         return pltpu.make_async_copy(tiles.at[k], out_ref.at[k], sems.at[k])
 
-    @pl.loop(0, slots)
+    @pl.loop(0, slots, unroll=2 if slots % 2 == 0 else 1)
     def _(k):
         slot = slots_ref[k]
         index = jnp.minimum(slot, NTILE - 1)
@@ -238,7 +238,10 @@
         ],
         compiler_params=pltpu.CompilerParams(vmem_limit_bytes=56 << 20),
         name="tiles",
-    )(tile_slots, coeffs)
+    )(
+        pltpu.with_memory_space_constraint(tile_slots, pltpu.HBM),
+        pltpu.with_memory_space_constraint(coeffs, pltpu.VMEM),
+    )
 
 
 def body(n, tm, snapshots, basis, tile_slots):

time: 28.5 us -> 27.1 us (0.951)
  Pallas kernels: 28.3 us -> 27 us
    pallas_call x1, Pallas kernels: 18.1 us -> 17.4 us  [coefficients(): pl.pallas_call(functools.partial(coeff_kernel, n, tm, chunks), out_shape=...]
    pallas_call x1, Pallas kernels: 10.2 us -> 9.58 us  [gram(): pl.pallas_call(tile_kernel, out_shape=jax.ShapeDtypeStruct((slots, BLK, B...]
where the time goes in v2:
time: 27.1 us; the launch traced here: 27 us
  Pallas kernels  27 us (100%)
    pallas_call x1, Pallas kernels, coefficients(): pl.pallas_call(functools.partial(coeff_kernel, n, tm, chunks), out_shape=...  17.4 us
    pallas_call x1, Pallas kernels, gram(): pl.pallas_call(tile_kernel, out_shape=jax.ShapeDtypeStruct((slots, BLK, B...  9.58 us

profile of v2, /device:TPU:0, one launch (start us, length us, event | category | flops | bytes accessed | tf_op | source)
XLA Modules:
  0.0 27.0 jit_solution(200748560654892523)
XLA Ops:
  0.0 17.4 %coeffs.1.coeff_ref = f32[1,192,128]{2,1,0:T(8,128)S(1)} custom-call(bf16[192,8192]{1,0:T(8,128)(2,1)} %bitcast.2, bf16[64,8192]{1,0:T(8,128)(2,1)} %bitcast.3), custom_call_target="tpu_custom_call" | custom-call | tf_op jit(solution)/shard_map/coeffs/pallas_call | solution.py:149
  17.4 9.6 %tiles.1 = f32[22,512,512]{2,1,0:T(8,128)} custom-call(s32[22]{0:T(128)} %slots_ref.1, f32[1,192,128]{2,1,0:T(8,128)S(1)} %coeffs.1.coeff_ref), custom_call_target="tpu_custom_call" | custom-call | tf_op jit(solution)/shard_map/tiles/pallas_call | solution.py:225

commit v3 on v2

--- a/solution.py
+++ b/solution.py
@@ -34,7 +34,6 @@
     total = n * tm
     s = lax.axis_index("space")
     t = lax.axis_index("tm")
-    me = s * tm + t
     width = snap_ref.shape[0]
     depth = basis_ref.shape[1] // chunks
     rows = HALF // n
@@ -48,18 +47,15 @@
         two.start()
         loads.append((one, two))
 
+    def turn(v, size):
+        return jnp.where(v >= size, v - size, v)
+
+    spaces = [s] + [turn(s + d, n) for d in range(1, n)]
+    times = [t] + [turn(t + e, tm) for e in range(1, tm)]
+    peers = [{"space": p, "tm": u} for u in times for p in spaces]
     barrier = pltpu.get_barrier_semaphore()
-
-    def greet(d, carry):
-        peer = lax.rem(me + d, total)
-        pl.semaphore_signal(
-            barrier, inc=1,
-            device_id={"space": lax.div(peer, tm), "tm": lax.rem(peer, tm)},
-            device_id_type=MESH,
-        )
-        return carry
-
-    lax.fori_loop(1, total, greet, 0)
+    for peer in peers[1:]:
+        pl.semaphore_signal(barrier, inc=1, device_id=peer, device_id_type=MESH)
 
     acc = jnp.zeros((R, width), jnp.float32)
     for k in range(chunks):
@@ -74,52 +70,36 @@
 
     pl.semaphore_wait(barrier, total - 1)
 
-    def scatter(d):
-        dst = lax.rem(s + d, n)
-        return pltpu.make_async_remote_copy(
-            src_ref=part.at[dst], dst_ref=recv.at[d],
+    scatters = [
+        pltpu.make_async_remote_copy(
+            src_ref=part.at[spaces[d]], dst_ref=recv.at[d],
             send_sem=send1.at[d], recv_sem=recv1.at[d],
-            device_id={"space": dst, "tm": t}, device_id_type=MESH,
+            device_id=peers[d], device_id_type=MESH,
         )
-
-    def start_scatter(d, carry):
-        scatter(d).start()
-        return carry
-
-    lax.fori_loop(1, n, start_scatter, 0)
-
-    def add(d, value):
-        scatter(d).wait_recv()
-        return value + recv[d]
-
-    gath[t, s] = lax.fori_loop(1, n, add, part[s])
-
-    def gather(d):
-        peer = lax.rem(me + d, total)
-        return pltpu.make_async_remote_copy(
+        for d in range(1, n)
+    ]
+    for one in scatters:
+        one.start()
+    value = part[s]
+    for d, one in enumerate(scatters):
+        one.wait_recv()
+        value = value + recv[d + 1]
+    gath[t, s] = value
+
+    gathers = [
+        pltpu.make_async_remote_copy(
             src_ref=gath.at[t, s], dst_ref=gath.at[t, s],
             send_sem=send2.at[d], recv_sem=recv2.at[d],
-            device_id={"space": lax.div(peer, tm), "tm": lax.rem(peer, tm)},
-            device_id_type=MESH,
+            device_id=peers[d], device_id_type=MESH,
         )
-
-    def start_gather(d, carry):
-        gather(d).start()
-        return carry
-
-    lax.fori_loop(1, total, start_gather, 0)
-
-    def end_scatter(d, carry):
-        scatter(d).wait_send()
-        return carry
-
-    lax.fori_loop(1, n, end_scatter, 0)
-
-    def end_gather(d, carry):
-        gather(d).wait_recv()
-        return carry
-
-    lax.fori_loop(1, total, end_gather, 0)
+        for d in range(1, total)
+    ]
+    for one in gathers:
+        one.start()
+    for one in scatters:
+        one.wait_send()
+    for one in gathers:
+        one.wait_recv()
 
     for u in range(tm):
         for q in range(n):
@@ -132,11 +112,8 @@
                 [b[:, h * width:(h + 1) * width] for b in blocks], axis=1
             )
 
-    def end_send(d, carry):
-        gather(d).wait_send()
-        return carry
-
-    lax.fori_loop(1, total, end_send, 0)
+    for one in gathers:
+        one.wait_send()
 
 
 def coefficients(n, tm, basis_t, snap_t):

time: 27.1 us -> 26.9 us (level)
  Pallas kernels: 27 us -> 26.7 us
where the time goes in v3:
time: 26.9 us; the launch traced here: 26.7 us
  Pallas kernels  26.7 us (99%)
    pallas_call x1, Pallas kernels, coefficients(): pl.pallas_call(functools.partial(coeff_kernel, n, tm, chunks), out_shape=...  17.2 us
    pallas_call x1, Pallas kernels, gram(): pl.pallas_call(tile_kernel, out_shape=jax.ShapeDtypeStruct((slots, BLK, B...  9.58 us

profile of v3, /device:TPU:0, one launch (start us, length us, event | category | flops | bytes accessed | tf_op | source)
XLA Modules:
  0.0 26.7 jit_solution(15759214601713617580)
XLA Ops:
  0.0 17.2 %coeffs.1.coeff_ref = f32[1,192,128]{2,1,0:T(8,128)S(1)} custom-call(bf16[192,8192]{1,0:T(8,128)(2,1)} %bitcast.2, bf16[64,8192]{1,0:T(8,128)(2,1)} %bitcast.3), custom_call_target="tpu_custom_call" | custom-call | tf_op jit(solution)/shard_map/coeffs/pallas_call | solution.py:126
  17.2 9.6 %tiles.1 = f32[22,512,512]{2,1,0:T(8,128)} custom-call(s32[22]{0:T(128)} %slots_ref.1, f32[1,192,128]{2,1,0:T(8,128)S(1)} %coeffs.1.coeff_ref), custom_call_target="tpu_custom_call" | custom-call | tf_op jit(solution)/shard_map/tiles/pallas_call | solution.py:202
